TPU v7x, 128 devices: a whole 4x4x4 slice. The times are simulated.
128 devices in a mesh: dp: 8 (over x, core), seq: 16 (over z, y).
Axes of the slice: x: 4, y: 4, z: 4, core: 2. Of those that a mesh axis runs over, the one named last changes fastest.
Arguments:
- tokens: bfloat16 [8, 12288, 2560], P('dp', 'seq'), may hold values from -6 to 6
- w_xbc: bfloat16 [2560, 2816], P(('dp', 'seq')), may hold values from -0.125 to 0.125
- conv_weight: float32 [4, 2816], replicated, may hold values from -3 to 3
- conv_bias: float32 [2816], replicated, may hold values from -2 to 2
- a_log: float32 [40], replicated, may hold values from -13 to -3
- dt_in: float32 [8, 40, 12288], P('dp', None, 'seq'), may hold values from -2 to 98304
- d_skip: float32 [40], replicated, may hold values from 0.5 to 1.5
- norm_gain: float32 [2560], replicated, may hold values from 0.25 to 1.75
Outputs:
- normed: bfloat16 [8, 12288, 2560], P('dp', 'seq')
All inputs are finite; a program needn't handle non-finite values.
Results may differ from a plain program's by a relative error of at most 0.012.
Values may be sent and summed in bfloat16 or wider, within the bound.
A program may use at most 128 MiB of HBM per device.

v0:
```python
import jax
import jax.numpy as jnp
from jax import lax
from jax.sharding import PartitionSpec as P

GROUP = 256


def passed_along(value, axis, by):
    length = lax.axis_size(axis)
    pairs = [(i, i + by) for i in range(length) if 0 <= i + by < length]
    return lax.ppermute(value, axis, pairs)


def prefix(value, axis, join, neutral):
    count, mine = (lax.axis_size(axis), lax.axis_index(axis))
    pieces = jax.tree.map(lambda part: lax.all_gather(part, axis), value)
    running = jax.tree.map(
        lambda part, zero: jnp.full_like(part, 0) + jnp.asarray(zero, part.dtype), value, neutral
    )

    def hop(position, running):
        longer = join(running, jax.tree.map(lambda part: part[position], pieces))
        return jax.tree.map(lambda new, old: jnp.where(position < mine, new, old), longer, running)

    return lax.fori_loop(0, count - 1, hop, running)


def block_state(x_block, b_block, dt_block, decay_block):
    heads = dt_block.shape[0]
    length = dt_block.shape[1]
    x_heads = x_block.astype(jnp.float32).reshape(length, heads, -1)
    cumul = jnp.cumsum(decay_block, axis=1)
    tail_weight = jnp.exp(cumul[:, -1:] - cumul) * dt_block
    weighted = tail_weight.T[:, :, None] * x_heads
    span_state = jnp.einsum(
        "jhp,jn->hpn", weighted, b_block.astype(jnp.float32), precision=lax.Precision.HIGH
    )
    return (span_state, cumul[:, -1])


def block_inner(x_block, b_block, c_block, dt_block, decay_block):
    heads = dt_block.shape[0]
    length = dt_block.shape[1]
    x_heads = x_block.astype(jnp.float32).reshape(length, heads, -1)
    cumul = jnp.cumsum(decay_block, axis=1)
    spread = cumul[:, :, None] - cumul[:, None, :]
    lower = jnp.arange(length)[:, None] >= jnp.arange(length)[None, :]
    decay_mat = jnp.exp(jnp.where(lower[None], spread, -jnp.inf))
    scores = jnp.dot(c_block, b_block.T, preferred_element_type=jnp.float32)
    mixing = decay_mat * scores[None] * dt_block[:, None, :]
    y_inner = jnp.einsum("hij,jhp->ihp", mixing, x_heads, precision=lax.Precision.HIGH)
    return (y_inner, cumul, x_heads)


def combine_carry(earlier, later):
    return (earlier[0] + later[0], jnp.exp(later[0])[:, None, None] * earlier[1] + later[1])


def local(tokens, w_xbc, conv_weight, conv_bias, a_log, dt_in, d_skip, norm_gain):
    token_rows = tokens[0]
    tok_count = token_rows.shape[0]
    heads = a_log.shape[0]
    width_x = norm_gain.shape[0]
    head_size = width_x // heads
    channels = w_xbc.shape[1]
    state_size = (channels - width_x) // 2
    kernel = conv_weight.shape[0]
    projected = jnp.dot(
        token_rows,
        lax.all_gather(w_xbc, ("dp", "seq"), axis=0, tiled=True),
        preferred_element_type=jnp.float32,
    )
    xbc = projected.astype(jnp.bfloat16)
    rim_rows = passed_along(xbc[tok_count - (kernel - 1) :], "seq", 1)
    padded = jnp.concatenate([rim_rows, xbc], axis=0)
    accum = conv_bias[None, :] + jnp.zeros((tok_count, channels), jnp.float32)
    for tap_index in range(kernel):
        accum = accum + conv_weight[tap_index][None, :] * padded[
            tap_index : tap_index + tok_count
        ].astype(jnp.float32)
    conv_out = jax.nn.silu(accum).astype(jnp.bfloat16)
    step_size = jax.nn.softplus(dt_in[0])
    log_decay = -jnp.exp(a_log)[:, None] * step_size
    blocks = tok_count // GROUP
    gain_heads = norm_gain.reshape(heads, head_size)[None]
    pieces = []
    own_state = jnp.zeros((heads, head_size, state_size), jnp.float32)
    own_decay = jnp.zeros((heads,), jnp.float32)
    for block_index in range(blocks):
        lo_row = block_index * GROUP
        block_rows = conv_out[lo_row : lo_row + GROUP]
        x_block = block_rows[:, :width_x]
        b_block = block_rows[:, width_x : width_x + state_size]
        c_block = block_rows[:, width_x + state_size :]
        dt_block = step_size[:, lo_row : lo_row + GROUP]
        decay_block = log_decay[:, lo_row : lo_row + GROUP]
        span_state, totals = block_state(x_block, b_block, dt_block, decay_block)
        own_state = jnp.exp(totals)[:, None, None] * own_state + span_state
        own_decay = own_decay + totals
        pieces.append((x_block, b_block, c_block, dt_block, decay_block, span_state, totals))
    identity = (jnp.zeros_like(own_decay), jnp.zeros_like(own_state))
    earlier_decay, incoming = prefix((own_decay, own_state), "seq", combine_carry, identity)
    state = incoming
    outputs = []
    for block_index in range(blocks):
        x_block, b_block, c_block, dt_block, decay_block, span_state, totals = pieces[block_index]
        y_inner, cumul, x_heads = block_inner(x_block, b_block, c_block, dt_block, decay_block)
        from_state = jnp.einsum(
            "in,hpn->ihp", c_block.astype(jnp.float32), state, precision=lax.Precision.HIGH
        )
        ssd = y_inner + jnp.exp(cumul).T[:, :, None] * from_state + d_skip[None, :, None] * x_heads
        mean_sq = jnp.mean(ssd * ssd, axis=-1, keepdims=True)
        scaled = ssd * lax.rsqrt(mean_sq + 1e-05) * gain_heads
        outputs.append(scaled.reshape(GROUP, width_x).astype(jnp.bfloat16))
        state = jnp.exp(totals)[:, None, None] * state + span_state
    return jnp.concatenate(outputs, axis=0)[None]


def solution(mesh):
    return jax.shard_map(
        local,
        mesh=mesh,
        in_specs=(
            P("dp", "seq", None),
            P(("dp", "seq"), None),
            P(),
            P(),
            P(),
            P("dp", None, "seq"),
            P(),
            P(),
        ),
        out_specs=P("dp", "seq", None),
        check_vma=False,
    )
```

profile of v0, /device:TPU:0, one launch (start us, length us, event | category | flops | bytes accessed | tf_op | source)
XLA Modules:
  0.0 367.4 jit_solution(12167026714870173154)
XLA Ops:
  8.0 1.0 compare_select_fusion
  13.2 80.3 %all-gather.8.cloned.1.call-done = bf16[128,20,2816]{2,1,0:T(8,128)(2,1)} async-done(((bf16[1,20,2816]{2,1,0:T(8,128)(2,1)}), bf16[128,20,2816]{2,1,0:T(8,128)(2,1)}) %all-gather.8.cloned.1.call-update) | async-done | bytes 14417936 | tf_op jit(solution)/shard_map/all_gather | solution.py:71
  93.5 20.5 %reshape.252 = bf16[2560,2816]{1,0:T(8,128)(2,1)} reshape(bf16[128,20,2816]{2,1,0:T(8,128)(2,1)} %all-gather.8.cloned.1.call-done) | data formatting | bytes 28835840
  114.0 16.4 %convolution_convert_fusion = bf16[768,2816]{1,0:T(8,128)(2,1)S(1)} fusion(bf16[2560,2816]{1,0:T(8,128)(2,1)} %reshape.252, bf16[1,768,2560]{2,1,0:T(8,128)(2,1)} %param.10), kind=kOutput, calls=%fused_computation.42 | convolution fusion | flops 11075125248 | bytes 22675456 | tf_op jit(solution)/shard_map/dot_general | solution.py:69
  130.5 3.4 collective-permute-start
  134.0 1.3 collective-permute-done
  135.3 6.3 %multiply_convert_fusion = bf16[768,2816]{1,0:T(8,128)(2,1)S(1)} fusion(bf16[768,2816]{1,0:T(8,128)(2,1)S(1)} %convolution_convert_fusion, bf16[3,2816]{1,0:T(4,128)(2,1)S(1)} %collective-permute-done, f32[2816]{0:T(1024)S(1)} %get-tuple-element.120, f32[2816]{0:T(1024)S(1)} %get-tuple-element.121, f32[2816]{0:T(1024)S(1)} %get-tuple-element.119, ...), kind=kLoop, calls=%fused_computation.21 | loop fusion | flops 56229888 | bytes 8723968 | tf_op jit(solution)/shard_map/convert_element_type | solution.py:82
  141.7 2.0 fusion.90
  143.7 0.8 copy-done
  144.5 1.6 copy.33
  146.1 2.9 copy.40
  149.0 1.5 copy.41
  150.5 1.8 fusion.40
  152.4 1.7 fusion.42
  154.1 1.0 copy-done.1
  155.1 2.9 fusion.52
  159.5 41.8 %all-reduce = f32[640]{0:T(1024)S(1)} all-reduce(f32[640]{0:T(1024)S(1)} %dynamic-update-slice), channel_id=2, replica_groups=mesh['dp'=8,'seq'=16] {'seq'}, use_global_device_ids=true, to_apply=%add | all-reduce | flops 640 | bytes 5120
  202.7 1.1 fusion.73
  203.8 1.1 fusion.76
  204.9 1.1 fusion.83
  206.0 86.1 %all-gather.6.cloned.1.call-done = f32[640,64,128]{2,1,0:T(8,128)} async-done(((f32[40,64,128]{2,1,0:T(8,128)}), f32[640,64,128]{2,1,0:T(8,128)}) %all-gather.6.cloned.1.call-update) | async-done | bytes 20971536 | tf_op jit(solution)/shard_map/all_gather | solution.py:17
  292.2 35.1 %while.14 = (s32[]{:T(128)}, f32[40,64,128]{2,1,0:T(8,128)S(1)}, s32[]{:T(128)}, f32[16,40]{1,0:T(8,128)}, f32[16,40,64,128]{3,2,1,0:T(8,128)}, /*index=5*/s32[]{:T(128)}, s32[]{:T(128)}) while((s32[]{:T(128)}, f32[40,64,128]{2,1,0:T(8,128)S(1)}, s32[]{:T(128)}, f32[16,40]{1,0:T(8,128)}, f32[16,40,64,128]{3,2,1,0:T(8,128)}, ...), condition=%wide.region_7.8_spmd.clone, body=%wide.region_6.7_spmd.clone.sunk | while | flops 1310724 | bytes 3932745 | solution.py:26
  292.8 1.6 fusion.99
  295.2 1.6 fusion.99
  297.5 1.6 fusion.99
  299.8 1.6 fusion.99
  302.2 1.6 fusion.99
  304.5 1.6 fusion.99
  306.8 1.6 fusion.99
  309.1 1.6 fusion.99
  311.5 1.6 fusion.99
  313.8 1.6 fusion.99
  316.1 1.6 fusion.99
  318.5 1.6 fusion.99
  320.8 1.6 fusion.99
  323.1 1.6 fusion.99
  325.4 1.6 fusion.99
  327.3 2.2 fusion.53
  329.5 1.7 fusion.60
  331.3 1.8 fusion.70
  333.2 5.3 %multiply_reduce_fusion = (f32[256,40]{0,1:T(8,128)S(1)}, f32[256,40,64]{0,2,1:T(8,128)S(1)}) fusion(bf16[256,40,64]{0,2,1:T(8,128)(2,1)S(1)} %bitcast.140, f32[40]{0:T(128)S(1)} %copy-done.21, f32[256,40,64]{0,2,1:T(8,128)S(1)} %fusion.53, f32[256,40]{0,1:T(8,128)S(1)} %copy-done.16, f32[40,256]{1,0:T(8,128)S(1)} %copy-done.15, ...), kind=kOutput, calls=%fused_computation.64 | convolution fusion | flops 1021696000 | bytes 7045280 | tf_op jit(solution)/shard_map/hij,jhp->ihp/dot_general | solution.py:52
  338.5 5.5 %multiply_reduce_fusion.1 = (f32[256,40]{0,1:T(8,128)S(1)}, f32[256,40,64]{0,2,1:T(8,128)S(1)}) fusion(bf16[256,40,64]{0,2,1:T(8,128)(2,1)S(1)} %bitcast.138, f32[40]{0:T(128)S(1)} %copy-done.21, f32[256,40,64]{0,2,1:T(8,128)S(1)} %fusion.60, f32[256,40]{0,1:T(8,128)S(1)} %copy-done.14, f32[40,256]{1,0:T(8,128)S(1)} %copy-done.13, ...), kind=kOutput, calls=%fused_computation.66 | convolution fusion | flops 1021696000 | bytes 7045280 | tf_op jit(solution)/shard_map/hij,jhp->ihp/dot_general | solution.py:52
  344.1 5.2 %multiply_reduce_fusion.2 = (f32[256,40]{0,1:T(8,128)S(1)}, f32[256,40,64]{0,2,1:T(8,128)S(1)}) fusion(bf16[256,40,64]{0,2,1:T(8,128)(2,1)S(1)} %bitcast.136, f32[40]{0:T(128)S(1)} %copy-done.21, f32[256,40,64]{0,2,1:T(8,128)S(1)} %fusion.70, f32[256,40]{0,1:T(8,128)S(1)} %copy-done.12, f32[40,256]{1,0:T(8,128)S(1)} %copy-done.11, ...), kind=kOutput, calls=%fused_computation.68 | convolution fusion | flops 1021696000 | bytes 7045280 | tf_op jit(solution)/shard_map/hij,jhp->ihp/dot_general | solution.py:52
  349.4 2.2 multiply_convert_fusion.3
  351.6 2.4 copy.42
  354.0 1.6 copy.43
  355.6 1.6 copy.44
  357.2 3.3 maximum_bitcast_fusion
  (99 shorter events, 18.5 us)
Async XLA Ops:
  6.5 87.0 %all-gather.8.cloned.1.call-start = ((), (), s32[]{:S(2)}) async-start(), calls=%async_computation.1 | async-start | bytes 17436672 | tf_op jit(solution)/shard_map/all_gather | solution.py:71
  7.3 284.9 %all-gather.6.cloned.1.call-start = ((), (), s32[]{:S(2)}) async-start(), calls=%async_computation | async-start | bytes 22282240 | tf_op jit(solution)/shard_map/all_gather | solution.py:17
  114.0 19.9 %copy-start.10 = (f32[4,2816]{1,0:T(4,128)S(1)}, f32[4,2816]{1,0:T(4,128)}, u32[]{:S(2)}) copy-start(f32[4,2816]{1,0:T(4,128)} %param.12) | copy-start | bytes 135172
  114.0 21.3 %copy-start.17 = (f32[2816]{0:T(1024)S(1)}, f32[2816]{0:T(1024)}, u32[]{:S(2)}) copy-start(f32[2816]{0:T(1024)} %param.13) | copy-start | bytes 33796
  130.5 4.9 %collective-permute-start = (bf16[3,2816]{1,0:T(4,128)(2,1)S(1)}, bf16[3,2816]{1,0:T(4,128)(2,1)S(1)}, u32[]{:S(2)}, u32[]{:S(2)}) collective-permute-start(bf16[3,2816]{1,0:T(4,128)(2,1)S(1)} %slice.143), channel_id=1, source_target_pairs={{0,1},{1,2},{2,3},{3,4},{4,5},{5,6},{6,7},{7,8},{8,9},{9,10},{10,1... | collective-permute-start | bytes 50696 | tf_op jit(solution)/shard_map/ppermute | solution.py:12
  134.0 20.1 %copy-start.20 = (f32[40]{0:T(128)}, f32[40]{0:T(128)S(1)}, u32[]{:S(2)}) copy-start(f32[40]{0:T(128)S(1)} %exp.81) | copy-start | bytes 484
  141.7 2.8 copy-start
  146.1 4.4 %copy-start.2 = (bf16[256,2560]{0,1:T(8,128)(2,1)}, bf16[256,2560]{0,1:T(8,128)(2,1)S(1)}, u32[]{:S(2)}) copy-start(bf16[256,2560]{0,1:T(8,128)(2,1)S(1)} %copy.33) | copy-start | bytes 3932164
  150.5 1.9 copy-start.4
  150.5 4.6 %copy-start.6 = (bf16[256,2560]{0,1:T(8,128)(2,1)S(1)}, bf16[256,2560]{0,1:T(8,128)(2,1)}, u32[]{:S(2)}) copy-start(bf16[256,2560]{0,1:T(8,128)(2,1)} %copy.41) | copy-start | bytes 3932164
  154.1 1.0 copy-start.1
  155.1 2.9 copy-start.22
  155.1 46.9 %copy-start.18 = (f32[2560]{0:T(1024)S(1)}, f32[2560]{0:T(1024)}, u32[]{:S(2)}) copy-start(f32[2560]{0:T(1024)} %param.17) | copy-start | bytes 30724
  327.3 2.2 copy-start.19
  331.2 1.8 copy-start.7
  331.2 1.8 copy-start.9
  331.2 1.8 copy-start.15
  331.3 1.8 copy-start.16
  331.3 1.8 copy-start.21
  333.1 5.3 %copy-start.5 = (bf16[256,2560]{0,1:T(8,128)(2,1)S(1)}, bf16[256,2560]{0,1:T(8,128)(2,1)}, u32[]{:S(2)}) copy-start(bf16[256,2560]{0,1:T(8,128)(2,1)} %copy.40) | copy-start | bytes 3932164
  333.1 5.3 %copy-start.13 = (f32[40,256]{1,0:T(8,128)S(1)}, f32[40,256]{1,0:T(8,128)}, u32[]{:S(2)}) copy-start(f32[40,256]{1,0:T(8,128)} %get-tuple-element.143) | copy-start | bytes 122884
  333.1 5.3 %copy-start.14 = (f32[256,40]{0,1:T(8,128)S(1)}, f32[256,40]{0,1:T(8,128)}, u32[]{:S(2)}) copy-start(f32[256,40]{0,1:T(8,128)} %get-tuple-element.152) | copy-start | bytes 122884
  338.5 5.6 %copy-start.3 = (bf16[256,2560]{0,1:T(8,128)(2,1)S(1)}, bf16[256,2560]{0,1:T(8,128)(2,1)}, u32[]{:S(2)}) copy-start(bf16[256,2560]{0,1:T(8,128)(2,1)} %copy-done.2) | copy-start | bytes 3932164
  338.5 5.6 %copy-start.11 = (f32[40,256]{1,0:T(8,128)S(1)}, f32[40,256]{1,0:T(8,128)}, u32[]{:S(2)}) copy-start(f32[40,256]{1,0:T(8,128)} %get-tuple-element.139) | copy-start | bytes 122884
  338.5 5.6 %copy-start.12 = (f32[256,40]{0,1:T(8,128)S(1)}, f32[256,40]{0,1:T(8,128)}, u32[]{:S(2)}) copy-start(f32[256,40]{0,1:T(8,128)} %get-tuple-element.150) | copy-start | bytes 122884
  355.6 1.6 copy-start.8
Sparse Core Ops, SparseCore 0:
  10.4 83.1 all-gather.7
  158.1 133.9 all-gather.5
where the time goes:
time: 370 us; the launch traced here: 367 us
  waiting for transfers between devices  168 us (45%)
  local copies, waits for them, and re-layouts  48.7 us (13%)
  matrix products  47.8 us (13%)
  other arithmetic  42.2 us (11%)
  blocking collectives  41.8 us (11%)
  between operations  14.5 us (4%)
    all_gather x1, waiting for transfers between devices, prefix(): pieces = jax.tree.map(lambda part: lax.all_gather(part, axis), value)  86.1 us
    all_gather x1, waiting for transfers between devices, local(): lax.all_gather(w_xbc, ('dp', 'seq'), axis=0, tiled=True)  80.3 us
    unnamed x1, blocking collectives  41.8 us
    select_n x15, other arithmetic, hop(): jnp.where(position < mine, new, old)  24.3 us
    unnamed x51, local copies, waits for them, and re-layouts  23.3 us
    dot_general x1, matrix products, local(): jnp.dot(token_rows, lax.all_gather(w_xbc, ('dp', 'seq'), axis=0, tiled=Tr...  16.4 us
    dot_general x3, matrix products, block_inner(): jnp.einsum('hij,jhp->ihp', mixing, x_heads, precision=lax.Precision.HIGH)  16 us
    exp x15, local copies, waits for them, and re-layouts, combine_carry(): jnp.exp(later[0])[:, None, None] * earlier[1] + later[1]  10.4 us
  transfers between devices with their start and end apart: 3, of which 3 were waited for; matrix products, arithmetic and copies ran while one was open for 3% of the time, Pallas kernels for 0%

commit v1 on v0

v1 whole, which is shorter than its diff:
```python
import functools
import math

import jax
import jax.numpy as jnp
from jax import lax
from jax.experimental import pallas as pl
from jax.experimental.pallas import tpu as pltpu
from jax.sharding import PartitionSpec as P

Q = 128
LOG2E = math.log2(math.e)
F32 = jnp.float32
BF16 = jnp.bfloat16


def dot(a, b, precision=None):
    return lax.dot_general(
        a, b, (((1,), (0,)), ((), ())), precision=precision, preferred_element_type=F32
    )


def conv_silu(work, cw, cb, rows, pad):
    taps = cw.shape[0]
    acc = cb
    for k in range(taps):
        acc = acc + cw[k : k + 1, :] * work[pl.ds(pad - (taps - 1) + k, rows), :]
    half = 0.5 * acc
    return half + half * jnp.tanh(half)


def project_kernel(pad, tok_hbm, rim_hbm, w_ref, cw_ref, cb_ref, out_ref, tok, work, sems):
    rows = out_ref.shape[0]

    @pl.when(pl.program_id(0) == 0)
    def _():
        first = pltpu.make_async_copy(rim_hbm, tok.at[pl.ds(0, pad)], sems.at[0])
        second = pltpu.make_async_copy(tok_hbm, tok.at[pl.ds(pad, rows)], sems.at[1])
        first.start()
        second.start()
        first.wait()
        second.wait()

    xbc = dot(tok[...], w_ref[...])
    work[...] = xbc.astype(BF16).astype(F32)
    out_ref[...] = conv_silu(work, cw_ref[...], cb_ref[...], rows, pad).astype(BF16)


def project(tokens, rim, w, conv_weight, conv_bias):
    rows, depth = tokens.shape
    channels = w.shape[1]
    pad = rim.shape[0]
    wide = 256
    return pl.pallas_call(
        functools.partial(project_kernel, pad),
        out_shape=jax.ShapeDtypeStruct((rows, channels), BF16),
        grid=(channels // wide,),
        in_specs=[
            pl.BlockSpec(memory_space=pl.ANY),
            pl.BlockSpec(memory_space=pl.ANY),
            pl.BlockSpec((depth, wide), lambda i: (0, i)),
            pl.BlockSpec((conv_weight.shape[0], wide), lambda i: (0, i)),
            pl.BlockSpec((1, wide), lambda i: (0, i)),
        ],
        out_specs=pl.BlockSpec((rows, wide), lambda i: (0, i)),
        scratch_shapes=[
            pltpu.VMEM((rows + pad, depth), BF16),
            pltpu.VMEM((rows + pad, wide), F32),
            pltpu.SemaphoreType.DMA((2,)),
        ],
    )(tokens, rim, w, conv_weight, conv_bias[None, :])


def prepare(dt_ref, a_ref, cum_t, row, tail_t, base_t):
    heads, rows = dt_ref.shape
    v = dt_ref[...]
    dt = jnp.maximum(v, 0.0) + jnp.log1p(jnp.exp(-jnp.abs(v)))
    log_dt = jnp.log2(dt)
    decay = (-LOG2E * jnp.exp(a_ref[...])) * dt
    upper = (
        lax.broadcasted_iota(jnp.int32, (Q, Q), 0) <= lax.broadcasted_iota(jnp.int32, (Q, Q), 1)
    ).astype(F32)
    base = jnp.zeros((heads, 1), F32)
    for c in range(rows // Q):
        span = slice(c * Q, (c + 1) * Q)
        cum = dot(decay[:, span], upper, lax.Precision.HIGHEST)
        total = cum[:, Q - 1 :]
        cum_t[c] = cum.T
        row[c] = cum - log_dt[:, span]
        tail_t[c] = jnp.exp2(total - cum + log_dt[:, span]).T
        base_t[c] = jnp.exp2(cum + base).T
        base = base + total
    return base


def pair_of(left, right):
    half = lax.broadcasted_iota(jnp.int32, (left.shape[0], 128), 1) < 64
    return jnp.where(half, left, right)


def states_pass(conv_ref, cum_t, tail_t, state, saved, width, n):
    blocks = cum_t.shape[0]
    state[...] = jnp.zeros_like(state)

    def step(c, carry):
        rows = pl.ds(pl.multiple_of(c * Q, Q), Q)
        b_t = conv_ref[rows, width : width + n].T
        last = cum_t[c, Q - 1 : Q, :]
        tail = tail_t[c]
        for pair in range(width // 128):
            h = 2 * pair
            cols = slice(pair * 128, (pair + 1) * 128)
            x = conv_ref[rows, cols].astype(F32)
            wx = (x * pair_of(tail[:, h : h + 1], tail[:, h + 1 : h + 2])).astype(BF16)
            old = state[:, cols]
            saved[c, :, cols] = old.astype(BF16)
            keep = jnp.exp2(pair_of(last[:, h : h + 1], last[:, h + 1 : h + 2]))
            state[:, cols] = keep * old + dot(b_t, wx)
        return carry

    lax.fori_loop(0, blocks, step, 0)


def inner_pass(conv_ref, cum_t, row, saved, skip_ref, part, width, n):
    blocks = cum_t.shape[0]
    lower = lax.broadcasted_iota(jnp.int32, (Q, Q), 0) >= lax.broadcasted_iota(jnp.int32, (Q, Q), 1)
    left = lax.broadcasted_iota(jnp.int32, (Q, 128), 1) < 64

    def step(c, carry):
        rows = pl.ds(pl.multiple_of(c * Q, Q), Q)
        b = conv_ref[rows, width : width + n]
        cm = conv_ref[rows, width + n :]
        scores = jnp.where(
            lower,
            lax.dot_general(cm, b, (((1,), (1,)), ((), ())), preferred_element_type=F32),
            0.0,
        )
        cum = cum_t[c]
        for pair in range(width // 128):
            cols = slice(pair * 128, (pair + 1) * 128)
            x = conv_ref[rows, cols]
            mixes = []
            own = []
            for h in (2 * pair, 2 * pair + 1):
                mine = jnp.broadcast_to(cum[:, h : h + 1], (Q, 128))
                spread = jnp.where(lower, mine - row[c, h : h + 1, :], -jnp.inf)
                mixes.append((jnp.exp2(spread) * scores).astype(BF16))
                own.append(mine)
            zero = jnp.zeros_like(x)
            stack = jnp.concatenate([jnp.where(left, x, zero), jnp.where(left, zero, x)], axis=0)
            y = dot(jnp.concatenate(mixes, axis=1), stack)
            y = y + jnp.exp2(jnp.where(left, own[0], own[1])) * dot(cm, saved[c, :, cols])
            part[rows, cols] = y + skip_ref[:, cols] * x.astype(F32)
        return carry

    lax.fori_loop(0, blocks, step, 0)


def final_pass(conv_ref, base_t, incoming, part, gain_ref, out_ref, width, n):
    blocks = base_t.shape[0]
    ri = lax.broadcasted_iota(jnp.int32, (128, 128), 0)
    ci = lax.broadcasted_iota(jnp.int32, (128, 128), 1)
    mean_of = jnp.where((ri < 64) == (ci < 64), 1.0 / 64, 0.0).astype(BF16)

    def step(c, carry):
        rows = pl.ds(pl.multiple_of(c * Q, Q), Q)
        cm = conv_ref[rows, width + n :]
        base = base_t[c]
        for pair in range(width // 128):
            h = 2 * pair
            cols = slice(pair * 128, (pair + 1) * 128)
            scale = pair_of(base[:, h : h + 1], base[:, h + 1 : h + 2])
            y = part[rows, cols] + scale * dot(cm, incoming[:, cols])
            mean_sq = dot((y * y).astype(BF16), mean_of)
            out_ref[rows, cols] = (y * lax.rsqrt(mean_sq + 1e-5) * gain_ref[:, cols]).astype(BF16)
        return carry

    lax.fori_loop(0, blocks, step, 0)


def ssd_kernel(width, n, conv_ref, dt_ref, a_ref, skip_ref,
               part, state_out, total_out, base_t, cum_t, row, tail_t, saved, state):
    total = prepare(dt_ref, a_ref, cum_t, row, tail_t, base_t)
    total_out[...] = jnp.broadcast_to(total, total_out.shape)
    states_pass(conv_ref, cum_t, tail_t, state, saved, width, n)
    state_out[...] = state[...].astype(BF16)
    inner_pass(conv_ref, cum_t, row, saved, skip_ref, part, width, n)


def final_kernel(width, n, conv_ref, base_t, incoming, part, gain_ref, out_ref):
    final_pass(conv_ref, base_t, incoming, part, gain_ref, out_ref, width, n)


def vmem():
    return pl.BlockSpec(memory_space=pltpu.VMEM)


def local(tokens, w_xbc, conv_weight, conv_bias, a_log, dt_in, d_skip, norm_gain):
    token_rows = tokens[0]
    rows = token_rows.shape[0]
    heads = a_log.shape[0]
    width = norm_gain.shape[0]
    size = width // heads
    channels = w_xbc.shape[1]
    n = (channels - width) // 2
    blocks = rows // Q
    pad = 16
    count = lax.axis_size("seq")
    rim = lax.ppermute(token_rows[rows - pad :], "seq", [(i, i + 1) for i in range(count - 1)])
    w = lax.all_gather(w_xbc, ("dp", "seq"), axis=0, tiled=True)
    conv_out = project(token_rows, rim, w, conv_weight, conv_bias)
    skip_row = jnp.repeat(d_skip, size)[None, :]
    part, state, total, base_t = pl.pallas_call(
        functools.partial(ssd_kernel, width, n),
        out_shape=(
            jax.ShapeDtypeStruct((rows, width), F32),
            jax.ShapeDtypeStruct((n, width), BF16),
            jax.ShapeDtypeStruct((heads, 128), F32),
            jax.ShapeDtypeStruct((blocks, Q, heads), F32),
        ),
        in_specs=[vmem()] * 4,
        out_specs=(vmem(),) * 4,
        scratch_shapes=[
            pltpu.VMEM((blocks, Q, heads), F32),
            pltpu.VMEM((blocks, heads, Q), F32),
            pltpu.VMEM((blocks, Q, heads), F32),
            pltpu.VMEM((blocks, n, width), BF16),
            pltpu.VMEM((n, width), F32),
        ],
    )(conv_out, dt_in[0], a_log[:, None], skip_row)
    pieces = lax.all_to_all(state.reshape(count, n // count, width), "seq", 0, 0)
    totals = lax.all_gather(total[:, 0], "seq")
    factor = jnp.repeat(jnp.exp2(totals), size, axis=1)
    running = jnp.zeros((n // count, width), F32)
    prefixes = []
    for i in range(count):
        prefixes.append(running.astype(BF16))
        running = factor[i][None, :] * running + pieces[i].astype(F32)
    incoming = lax.all_to_all(jnp.stack(prefixes), "seq", 0, 0).reshape(n, width)
    out = pl.pallas_call(
        functools.partial(final_kernel, width, n),
        out_shape=jax.ShapeDtypeStruct((rows, width), BF16),
        in_specs=[vmem()] * 5,
        out_specs=vmem(),
    )(conv_out, base_t, incoming, part, norm_gain[None, :])
    return out[None]


def solution(mesh):
    return jax.shard_map(
        local,
        mesh=mesh,
        in_specs=(
            P("dp", "seq", None),
            P(("dp", "seq"), None),
            P(),
            P(),
            P(),
            P("dp", None, "seq"),
            P(),
            P(),
        ),
        out_specs=P("dp", "seq", None),
        check_vma=False,
    )
```

time: 370 us -> 257 us (0.69)
  waiting for transfers between devices: 168 us -> 88.6 us
  Pallas kernels: 0 us -> 57.2 us
  matrix products: 47.8 us -> 0 us
  other arithmetic: 42.2 us -> 9.73 us
  local copies, waits for them, and re-layouts: 48.7 us -> 31.8 us
  starting transfers between devices: 3.43 us -> 13.8 us
    all_gather x2 -> x1, waiting for transfers between devices: 166 us -> 77.7 us  [local(): w = lax.all_gather(w_xbc, ('dp', 'seq'), axis=0, tiled=True)]
    pallas_call x0 -> x3, Pallas kernels: none -> 57.2 us  [the longest x1 23.6 us: project(): pl.pallas_call(functools.partial(project_kernel, pad), out_shape=jax.Shap...]
    dot_general x13 -> x0, matrix products: 47.8 us -> none  [the longest x1 16.4 us: local(): jnp.dot(token_rows, lax.all_gather(w_xbc, ('dp', 'seq'), axis=0, tiled=Tr...]
    select_n x16 -> x0, other arithmetic: 25.3 us -> none  [the longest x15 24.3 us: hop(): jnp.where(position < mine, new, old)]
    exp x17 -> x0, local copies, waits for them, and re-layouts: 10.4 us -> none  [the longest x15 10.4 us: combine_carry(): jnp.exp(later[0])[:, None, None] * earlier[1] + later[1]]
    all_to_all x0 -> x2, starting transfers between devices: none -> 10.2 us  [the longest x1 6.62 us: local(): lax.all_to_all(state.reshape(count, n // count, width), 'seq', 0, 0)]
    all_to_all x0 -> x2, waiting for transfers between devices: none -> 10.2 us  [the longest x1 10.2 us: local(): lax.all_to_all(jnp.stack(prefixes), 'seq', 0, 0).reshape(n, width)]
    unnamed x1 -> x14, other arithmetic: 0.01 us -> 9 us
  transfers between devices with their start and end apart: 3 -> 4, of which waited for: 3 -> 2; matrix products, arithmetic and copies ran while one was open for 3% -> 12% of each run, Pallas kernels for 0% -> 0%
where the time goes in v1:
time: 257 us; the launch traced here: 256 us
  waiting for transfers between devices  88.6 us (34%)
  Pallas kernels  57.2 us (22%)
  blocking collectives  40.7 us (16%)
  local copies, waits for them, and re-layouts  31.8 us (12%)
  between operations  14.2 us (6%)
  starting transfers between devices  13.8 us (5%)
  other arithmetic  9.73 us (4%)
    all_gather x1, waiting for transfers between devices, local(): w = lax.all_gather(w_xbc, ('dp', 'seq'), axis=0, tiled=True)  77.7 us
    unnamed x1, blocking collectives  40.7 us
    pallas_call x1, Pallas kernels, project(): pl.pallas_call(functools.partial(project_kernel, pad), out_shape=jax.Shap...  23.6 us
    unnamed x13, local copies, waits for them, and re-layouts  23.3 us
    pallas_call x1, Pallas kernels, local(): pl.pallas_call(functools.partial(ssd_kernel, width, n), out_shape=(jax.Sh...  20.8 us
    pallas_call x1, Pallas kernels, local(): pl.pallas_call(functools.partial(final_kernel, width, n), out_shape=jax.S...  12.7 us
    all_to_all x1, waiting for transfers between devices, local(): lax.all_to_all(jnp.stack(prefixes), 'seq', 0, 0).reshape(n, width)  10.2 us
    unnamed x14, other arithmetic  9 us
  transfers between devices with their start and end apart: 4, of which 2 were waited for; matrix products, arithmetic and copies ran while one was open for 12% of the time, Pallas kernels for 0%

profile of v1, /device:TPU:0, one launch (start us, length us, event | category | flops | bytes accessed | tf_op | source)
XLA Modules:
  0.0 256.0 jit_solution(17250062510629934864)
XLA Ops:
  6.5 0.7 all-gather.4.cloned.1.call-update
  7.3 0.9 slice_bitcast_fusion
  8.2 3.6 %collective-permute-start = (bf16[16,2560]{1,0:T(8,128)(2,1)S(1)}, bf16[16,2560]{1,0:T(8,128)(2,1)S(1)}, u32[]{:S(2)}, u32[]{:S(2)}) collective-permute-start(bf16[16,2560]{1,0:T(8,128)(2,1)S(1)} %slice_bitcast_fusion), channel_id=1, source_target_pairs={{0,1},{1,2},{2,3},{3,4},{4,5},{5,6},{6,7},{7,8},{8,9},{9,10},{10,1... | collective-permute-start | bytes 245768 | tf_op jit(solution)/shard_map/ppermute | solution.py:209
  11.7 1.3 broadcast_in_dim.77.cb_ref
  13.1 0.7 broadcast_in_dim.79
  13.8 0.7 broadcast_in_dim_reshape.3.skip_ref
  14.5 1.3 copy.11.a_ref
  15.8 77.7 %all-gather.4.cloned.1.call-done = bf16[128,20,2816]{2,1,0:T(8,128)(2,1)} async-done(((bf16[1,20,2816]{2,1,0:T(8,128)(2,1)}), bf16[128,20,2816]{2,1,0:T(8,128)(2,1)}) %all-gather.4.cloned.1.call-update) | async-done | bytes 14417936 | tf_op jit(solution)/shard_map/all_gather | solution.py:210
  93.5 20.2 %reshape.819.w_ref = bf16[2560,2816]{1,0:T(8,128)(2,1)} reshape(bf16[128,20,2816]{2,1,0:T(8,128)(2,1)} %all-gather.4.cloned.1.call-done) | data formatting | bytes 28835840
  113.7 0.6 copy-done.1
  114.4 23.6 %shard_map.82.conv_ref = bf16[768,2816]{1,0:T(8,128)(2,1)} custom-call(bf16[768,2560]{1,0:T(8,128)(2,1)} %bitcast.10, bf16[16,2560]{1,0:T(8,128)(2,1)} %copy-done.1, bf16[2560,2816]{1,0:T(8,128)(2,1)} %reshape.819.w_ref, f32[4,2816]{1,0:T(4,128)} %cw_ref.1, f32[1,2816]{1,0:T(1,128)} %broadcast_in_dim.77.cb_ref), custom_call_target="tpu_custom_call" | custom-call | tf_op jit(solution)/shard_map/pallas_call | solution.py:54
  138.0 20.8 %shard_map.83 = (f32[768,2560]{1,0:T(8,128)}, bf16[128,2560]{1,0:T(8,128)(2,1)}, f32[40,128]{1,0:T(8,128)}, f32[6,128,40]{2,1,0:T(8,128)}) custom-call(bf16[768,2816]{1,0:T(8,128)(2,1)} %shard_map.82.conv_ref, f32[40,768]{1,0:T(8,128)} %bitcast.14, f32[40,1]{1,0:T(8,128)} %copy.11.a_ref, f32[1,2560]{1,0:T(1,128)} %broadcast_in_dim_reshape.3.skip_ref), custom_call_target="tpu_custom_call" | custom-call | tf_op jit(solution)/shard_map/pallas_call | solution.py:213
  158.9 6.6 %all-to-all-start = ((bf16[16,8,2560]{2,1,0:T(8,128)(2,1)}), bf16[16,8,2560]{2,1,0:T(8,128)(2,1)S(1)}, u32[]{:S(2)}, u32[]{:S(2)}) async-start(bf16[16,8,2560]{2,1,0:T(8,128)(2,1)} %bitcast.12), calls=%async_computation | async-start | bytes 1310720 | tf_op jit(solution)/shard_map/all_to_all | solution.py:231
  165.5 0.6 constant_dynamic-update-slice_fusion
  166.1 0.7 dynamic-slice
  167.5 0.8 slice_reduce_fusion
  168.3 0.2 dynamic-update-slice
  168.6 40.7 %all-reduce = f32[640]{0:T(1024)S(1)} all-reduce(f32[640]{0:T(1024)S(1)} %dynamic-update-slice), channel_id=2, replica_groups=mesh['dp'=8,'seq'=16] {'seq'}, use_global_device_ids=true, to_apply=%add | all-reduce | flops 640 | bytes 5120
  209.3 0.1 fusion.17
  209.4 0.1 mul.235
  209.6 0.1 broadcast_in_dim.83
  209.7 0.1 broadcast_in_dim.85
  209.9 0.1 broadcast_in_dim.87
  210.0 0.1 broadcast_in_dim.89
  210.1 0.1 broadcast_in_dim.91
  210.3 0.1 broadcast_in_dim.93
  210.4 0.1 broadcast_in_dim.95
  210.9 0.1 broadcast_in_dim.101
  211.5 0.7 fusion.15
  212.2 0.6 fusion.14
  212.9 0.6 convert_dynamic-update-slice_fusion.5
  213.5 0.7 fusion.13
  214.1 0.7 convert_dynamic-update-slice_fusion.4
  214.8 0.6 fusion.12
  215.5 0.6 convert_dynamic-update-slice_fusion.3
  216.1 0.6 fusion.11
  216.7 0.6 convert_dynamic-update-slice_fusion.2
  217.4 0.6 fusion.10
  218.0 0.6 convert_dynamic-update-slice_fusion.1
  218.6 0.6 fusion.9
  219.3 0.6 convert_dynamic-update-slice_fusion
  219.9 0.6 fusion.8
  220.5 0.6 fusion.16
  221.2 3.6 %all-to-all-start.1 = ((bf16[16,8,2560]{2,1,0:T(8,128)(2,1)}), bf16[16,8,2560]{2,1,0:T(8,128)(2,1)S(1)}, u32[]{:S(2)}, u32[]{:S(2)}) async-start(bf16[16,8,2560]{2,1,0:T(8,128)(2,1)} %fusion.16), calls=%async_computation.1 | async-start | bytes 1310720 | tf_op jit(solution)/shard_map/all_to_all | solution.py:239
  224.8 0.6 broadcast_in_dim.110.gain_ref
  225.4 10.2 %all-to-all-done.1 = bf16[16,8,2560]{2,1,0:T(8,128)(2,1)S(1)} async-done(((bf16[16,8,2560]{2,1,0:T(8,128)(2,1)}), bf16[16,8,2560]{2,1,0:T(8,128)(2,1)S(1)}, u32[]{:S(2)}, u32[]{:S(2)}) %all-to-all-start.1) | async-done | bytes 655392 | tf_op jit(solution)/shard_map/all_to_all | solution.py:239
  235.6 0.9 copy-done
  236.4 12.7 %shard_map.84 = bf16[768,2560]{1,0:T(8,128)(2,1)} custom-call(bf16[768,2816]{1,0:T(8,128)(2,1)} %shard_map.82.conv_ref, f32[6,128,40]{2,1,0:T(8,128)} %get-tuple-element.9.base_t, bf16[128,2560]{1,0:T(8,128)(2,1)} %bitcast.11, f32[768,2560]{1,0:T(8,128)} %get-tuple-element.12.part, f32[1,2560]{1,0:T(1,128)} %broadcast_in_dim.110.gain_ref), custom_call_target="tpu_custom_call" | custom-call | tf_op jit(solution)/shard_map/pallas_call | solution.py:240
  (32 shorter events, 1.5 us)
Async XLA Ops:
  6.5 87.0 %all-gather.4.cloned.1.call-start = ((), (), s32[]{:S(2)}) async-start(), calls=%async_computation.2 | async-start | bytes 17436672 | tf_op jit(solution)/shard_map/all_gather | solution.py:210
  8.2 105.6 %collective-permute-start = (bf16[16,2560]{1,0:T(8,128)(2,1)S(1)}, bf16[16,2560]{1,0:T(8,128)(2,1)S(1)}, u32[]{:S(2)}, u32[]{:S(2)}) collective-permute-start(bf16[16,2560]{1,0:T(8,128)(2,1)S(1)} %slice_bitcast_fusion), channel_id=1, source_target_pairs={{0,1},{1,2},{2,3},{3,4},{4,5},{5,6},{6,7},{7,8},{8,9},{9,10},{10,1... | collective-permute-start | bytes 245768 | tf_op jit(solution)/shard_map/ppermute | solution.py:209
  113.7 0.6 copy-start.1
  138.0 28.1 %copy-start.3 = (u32[128]{0:T(128)S(1)}, u32[128]{0:T(128)}, u32[]{:S(2)}) copy-start(u32[128]{0:T(128)} %constant.11) | copy-start | bytes 1540
  158.9 65.9 %copy-start.2 = (f32[2560]{0:T(1024)S(1)}, f32[2560]{0:T(1024)}, u32[]{:S(2)}) copy-start(f32[2560]{0:T(1024)} %param.15) | copy-start | bytes 30724
  158.9 52.6 %all-to-all-start = ((bf16[16,8,2560]{2,1,0:T(8,128)(2,1)}), bf16[16,8,2560]{2,1,0:T(8,128)(2,1)S(1)}, u32[]{:S(2)}, u32[]{:S(2)}) async-start(bf16[16,8,2560]{2,1,0:T(8,128)(2,1)} %bitcast.12), calls=%async_computation | async-start | bytes 1310720 | tf_op jit(solution)/shard_map/all_to_all | solution.py:231
  221.2 14.4 %all-to-all-start.1 = ((bf16[16,8,2560]{2,1,0:T(8,128)(2,1)}), bf16[16,8,2560]{2,1,0:T(8,128)(2,1)S(1)}, u32[]{:S(2)}, u32[]{:S(2)}) async-start(bf16[16,8,2560]{2,1,0:T(8,128)(2,1)} %fusion.16), calls=%async_computation.1 | async-start | bytes 1310720 | tf_op jit(solution)/shard_map/all_to_all | solution.py:239
  235.6 0.9 copy-start
Sparse Core Ops, SparseCore 0:
  10.3 83.0 all-gather.3
